TPU v7x, 128 devices: a whole 4x4x4 slice. The times are simulated.
128 devices in a mesh: aa: 16 (over x, z), ba: 8 (over y, core).
Axes of the slice: x: 4, y: 4, z: 4, core: 2. Of those that a mesh axis runs over, the one named last changes fastest.
Arguments:
- tokens: bfloat16 [16384, 1024], P(('aa', 'ba')), may hold values from -24 to 24, as said below
- attn_gain: float32 [1024], replicated, may hold values from 0.25 to 1.75
- w_query: bfloat16 [1024, 1024], replicated, may hold values from -0.1875 to 0.1875
- w_key: bfloat16 [1024, 1024], replicated, may hold values from -0.1875 to 0.1875
- w_value: bfloat16 [1024, 1024], replicated, may hold values from -0.1875 to 0.1875
- head_gain: float32 [1024], P('ba'), may hold values from 0.25 to 1.75
- w_output: bfloat16 [1024, 1024], replicated, may hold values from -0.1875 to 0.1875
- mlp_gain: float32 [1024], replicated, may hold values from 0.25 to 1.75
- w_in: bfloat16 [1024, 4096], replicated, may hold values from -0.1875 to 0.1875
- w_out: bfloat16 [4096, 1024], replicated, may hold values from -0.09375 to 0.09375
Outputs:
- attended: bfloat16 [16384, 1024], P(('aa', 'ba'))
- result: bfloat16 [16384, 1024], P(('aa', 'ba'))
Inputs may be any that keep to these rules, and one draw needn't show every extreme that they name: `tokens`: entries have magnitude at most 24.
All inputs are finite; a program needn't handle non-finite values.
Results may differ from a plain program's by a relative error of at most 0.013.
Values may be sent and summed in bfloat16 or wider, within the bound.
No kernel may reach another device: no remote copies, remote signals or barrier semaphores. Data moves between devices by JAX's collectives and lax.ppermute only.
A program may use at most 128 MiB of HBM per device.

v0:
```python
import jax
import jax.numpy as jnp
from jax import lax
from jax.sharding import Mesh
from jax.sharding import PartitionSpec as P

D = 1024
H = 16
AA = ("aa_0", "aa_1")
AA_BA = ("aa_0", "aa_1", "ba")


def neutral_like(shard, identity):
    return jnp.zeros_like(shard) + jnp.asarray(identity, shard.dtype)


def prefix_by_axis(shard, axes, combine, identity):
    before = start = neutral_like(shard, identity)
    subtotal = shard
    for axis in reversed(axes):
        length, index = (lax.axis_size(axis), lax.axis_index(axis))
        pieces = lax.all_gather(subtotal.astype(jnp.bfloat16), axis)
        inside, subtotal = (start, start)
        for k in range(length):
            passed = k < index
            subtotal = combine(subtotal, pieces[k].astype(shard.dtype))
            inside = jnp.where(passed, subtotal, inside)
        before = combine(inside, before)
    return before


def rms_scale(matrix, scale_vec):
    matrix = matrix.astype(jnp.float32)
    return matrix * lax.rsqrt(jnp.mean(matrix * matrix, axis=-1, keepdims=True) + 1e-05) * scale_vec


def outer_features(vectors):
    length, head_count, head_size = vectors.shape
    return (vectors[..., :, None] * vectors[..., None, :]).reshape(
        length, head_count, head_size * head_size
    )


def features(vectors):
    return outer_features(vectors).astype(jnp.bfloat16)


def add_states(earlier_state, later_state):
    return earlier_state + later_state


def body(tokens, attn_gain, w_query, w_key, w_value, head_gain, w_output, mlp_gain, w_in, w_out):
    normed = rms_scale(tokens, attn_gain).astype(jnp.bfloat16)
    query_loc = jnp.dot(normed, w_query, preferred_element_type=jnp.float32).astype(jnp.bfloat16)
    keys_loc = jnp.dot(normed, w_key, preferred_element_type=jnp.float32).astype(jnp.bfloat16)
    values_loc = jnp.dot(normed, w_value, preferred_element_type=jnp.float32).astype(jnp.bfloat16)
    queries, keys, values = (
        lax.all_to_all(query_loc, "ba", split_axis=1, concat_axis=0, tiled=True),
        lax.all_to_all(keys_loc, "ba", split_axis=1, concat_axis=0, tiled=True),
        lax.all_to_all(values_loc, "ba", split_axis=1, concat_axis=0, tiled=True),
    )
    head_size = D // H
    length = queries.shape[0]
    head_count = queries.shape[1] // head_size
    block_len = min(512, length)
    blocks = length // block_len

    def shaped(matrix):
        return matrix.reshape(blocks, block_len, head_count, head_size)

    causal = jnp.arange(block_len)[:, None] >= jnp.arange(block_len)[None, :]

    def local_pass(carry_state, block_in):
        query_blk, key_blk, value_blk = block_in
        scores = jnp.einsum("ihd,jhd->hij", query_blk, key_blk, preferred_element_type=jnp.float32)
        weights = jnp.where(causal[None], scores * scores, 0.0).astype(jnp.bfloat16)
        inside = jnp.einsum("hij,jhd->ihd", weights, value_blk, preferred_element_type=jnp.float32)
        key_feat = features(key_blk.astype(jnp.float32))
        grown_state = carry_state + jnp.einsum(
            "jhf,jhd->fhd", key_feat, value_blk, preferred_element_type=jnp.float32
        )
        return (grown_state, (inside, carry_state))

    feat_count = features(jnp.zeros((1, 1, head_size), jnp.float32)).shape[-1]
    start_state = jnp.zeros((feat_count, head_count, head_size), jnp.float32)
    local_total, (inside_all, before_all) = lax.scan(
        local_pass, start_state, (shaped(queries), shaped(keys), shaped(values))
    )
    flat_total = local_total.reshape(feat_count, head_count * head_size)
    earlier = prefix_by_axis(flat_total, AA, add_states, jnp.zeros_like(flat_total))
    earlier = earlier.reshape(feat_count, head_count, head_size)

    def apply_pass(block_in):
        query_blk, inside, before = block_in
        query_feat = features(query_blk.astype(jnp.float32))
        state_bf = (before + earlier).astype(jnp.bfloat16)
        carried = jnp.einsum(
            "ihf,fhd->ihd", query_feat, state_bf, preferred_element_type=jnp.float32
        )
        return inside + carried

    numerator = lax.map(apply_pass, (shaped(queries), inside_all, before_all)).reshape(
        length, head_count, head_size
    )
    scaled = numerator * lax.rsqrt(jnp.mean(numerator * numerator, axis=-1, keepdims=True) + 1e-05)
    scaled = scaled * head_gain.reshape(head_count, head_size)
    attended_heads = scaled.reshape(length, head_count * head_size).astype(jnp.bfloat16)
    attended = lax.all_to_all(attended_heads, "ba", split_axis=0, concat_axis=1, tiled=True)
    stream = (
        tokens.astype(jnp.float32) + jnp.dot(attended, w_output, preferred_element_type=jnp.float32)
    ).astype(jnp.bfloat16)
    normed_mlp = rms_scale(stream, mlp_gain).astype(jnp.bfloat16)
    hidden = jax.nn.gelu(
        jnp.dot(normed_mlp, w_in, preferred_element_type=jnp.float32), approximate=True
    ).astype(jnp.bfloat16)
    result = (
        stream.astype(jnp.float32) + jnp.dot(hidden, w_out, preferred_element_type=jnp.float32)
    ).astype(jnp.bfloat16)
    return (attended, result)


def solution(mesh):
    finer = Mesh(mesh.devices.reshape(4, 4, mesh.shape["ba"]), ("aa_0", "aa_1", "ba"))
    placed = (P(AA_BA, None), P(), P(), P(), P(), P("ba"), P(), P(), P(), P())
    return jax.shard_map(
        body,
        mesh=finer,
        in_specs=placed,
        out_specs=(P(AA_BA, None), P(AA_BA, None)),
        check_vma=False,
    )
```

profile of v0, /device:TPU:1, one launch (start us, length us, event | category | flops | bytes accessed | tf_op | source)
XLA Modules:
  0.0 256.1 jit_solution(17409837083859735016)
XLA Ops:
  11.5 6.0 %all-to-all-start.2 = ((bf16[128,8,128]{0,2,1:T(8,128)(2,1)}), bf16[128,8,128]{0,2,1:T(8,128)(2,1)S(1)}, u32[]{:S(2)}, u32[]{:S(2)}) async-start(bf16[128,8,128]{0,2,1:T(8,128)(2,1)} %bitcast.11), calls=%async_computation.2 | async-start | bytes 524288 | tf_op jit(solution)/shard_map/all_to_all | solution.py:58
  20.4 3.5 %all-to-all-done.2 = bf16[128,8,128]{0,2,1:T(8,128)(2,1)S(1)} async-done(((bf16[128,8,128]{0,2,1:T(8,128)(2,1)}), bf16[128,8,128]{0,2,1:T(8,128)(2,1)S(1)}, u32[]{:S(2)}, u32[]{:S(2)}) %all-to-all-start.2) | async-done | bytes 262176 | tf_op jit(solution)/shard_map/all_to_all | solution.py:58
  23.9 4.4 %all-to-all-start = ((bf16[128,8,128]{0,2,1:T(8,128)(2,1)}), bf16[128,8,128]{0,2,1:T(8,128)(2,1)S(1)}, u32[]{:S(2)}, u32[]{:S(2)}) async-start(bf16[128,8,128]{0,2,1:T(8,128)(2,1)} %bitcast.7), calls=%async_computation | async-start | bytes 524288 | tf_op jit(solution)/shard_map/all_to_all | solution.py:60
  31.2 3.6 %all-to-all-done = bf16[128,8,128]{0,2,1:T(8,128)(2,1)S(1)} async-done(((bf16[128,8,128]{0,2,1:T(8,128)(2,1)}), bf16[128,8,128]{0,2,1:T(8,128)(2,1)S(1)}, u32[]{:S(2)}, u32[]{:S(2)}) %all-to-all-start) | async-done | bytes 262176 | tf_op jit(solution)/shard_map/all_to_all | solution.py:60
  34.8 4.4 %all-to-all-start.1 = ((bf16[128,8,128]{0,2,1:T(8,128)(2,1)}), bf16[128,8,128]{0,2,1:T(8,128)(2,1)S(1)}, u32[]{:S(2)}, u32[]{:S(2)}) async-start(bf16[128,8,128]{0,2,1:T(8,128)(2,1)} %bitcast.9), calls=%async_computation.1 | async-start | bytes 524288 | tf_op jit(solution)/shard_map/all_to_all | solution.py:59
  40.5 5.1 %all-to-all-done.1 = bf16[128,8,128]{0,2,1:T(8,128)(2,1)S(1)} async-done(((bf16[128,8,128]{0,2,1:T(8,128)(2,1)}), bf16[128,8,128]{0,2,1:T(8,128)(2,1)S(1)}, u32[]{:S(2)}, u32[]{:S(2)}) %all-to-all-start.1) | async-done | bytes 262176 | tf_op jit(solution)/shard_map/all_to_all | solution.py:59
  46.7 25.1 %while.26 = (s32[]{:T(128)}, f32[4096,2,64]{0,2,1:T(8,128)}, f32[2,512,2,64]{1,3,2,0:T(8,128)S(1)}, f32[2,4096,2,64]{1,3,2,0:T(8,128)}, bf16[2,512,2,64]{1,3,2,0...) while((s32[]{:T(128)}, f32[4096,2,64]{0,2,1:T(8,128)}, ...), condition=%wide.region_2.3_spmd.clone, body=%wide.region_1.2_spmd.clone.sunk | while | flops 682950656 | bytes 43911844 | solution.py:86
  49.2 3.3 %multiply_convert_fusion.11 = bf16[512,2,64,64]{0,3,2,1:T(8,128)(2,1)S(1)} fusion(f32[512,2,64]{0,2,1:T(8,128)S(1)} %bitcast_convert_fusion.5), kind=kLoop, calls=%fused_computation.10.clone.1 | loop fusion | flops 8388608 | bytes 8650752 | tf_op jit(solution)/shard_map/while/body/eval_jaxpr/convert_element_type | solution.py:45
  52.5 2.8 %fusion.100 = f32[4096,2,64]{0,2,1:T(8,128)S(1)} fusion(bf16[512,2,4096]{0,2,1:T(8,128)(2,1)S(1)} %bitcast.123, f32[4096,2,64]{0,2,1:T(8,128)S(1)} %copy-done.1, pred[]{:T(512)S(6)} %compare.3, bf16[2,512,2,64]{1,3,2,0:T(8,128)(2,1)S(1)} %get-tuple-element.310, s32[]{:T(128)} %get-tuple-element.297), kind=kOutput, calls=%fused_computation.12.clone.1 | convolution fusion | flops 537919488 | bytes 12713989 | tf_op jit(solution)/shard_map/while/body/eval_jaxpr/jhf,jhd->fhd/dot_general | solution.py:79
  58.5 3.1 %bitcast_dynamic-update-slice_fusion.2 = f32[2,4096,2,64]{1,3,2,0:T(8,128)} fusion(f32[2,4096,2,64]{1,3,2,0:T(8,128)} %get-tuple-element.300, s32[]{:T(128)} %get-tuple-element.297, f32[4096,2,64]{0,2,1:T(8,128)} %get-tuple-element.298, pred[]{:T(512)S(6)} %compare.3), kind=kLoop, calls=%fused_computation.13.clone.1 | loop fusion | flops 524288 | bytes 4194817 | tf_op jit(solution)/shard_map/while/body/jit(dynamic_update_index_in_dim)/dynamic_update_slice | solution.py:86
  62.5 3.3 %multiply_convert_fusion.11 = bf16[512,2,64,64]{0,3,2,1:T(8,128)(2,1)S(1)} fusion(f32[512,2,64]{0,2,1:T(8,128)S(1)} %bitcast_convert_fusion.5), kind=kLoop, calls=%fused_computation.10.clone.1 | loop fusion | flops 8388608 | bytes 8650752 | tf_op jit(solution)/shard_map/while/body/eval_jaxpr/convert_element_type | solution.py:45
  65.8 2.8 %fusion.100 = f32[4096,2,64]{0,2,1:T(8,128)S(1)} fusion(bf16[512,2,4096]{0,2,1:T(8,128)(2,1)S(1)} %bitcast.123, f32[4096,2,64]{0,2,1:T(8,128)S(1)} %copy-done.1, pred[]{:T(512)S(6)} %compare.3, bf16[2,512,2,64]{1,3,2,0:T(8,128)(2,1)S(1)} %get-tuple-element.310, s32[]{:T(128)} %get-tuple-element.297), kind=kOutput, calls=%fused_computation.12.clone.1 | convolution fusion | flops 537919488 | bytes 12713989 | tf_op jit(solution)/shard_map/while/body/eval_jaxpr/jhf,jhd->fhd/dot_general | solution.py:79
  71.8 2.9 %convert_element_type.145 = bf16[4096,2,64]{0,2,1:T(8,128)(2,1)} convert(f32[4096,2,64]{0,2,1:T(8,128)} %get-tuple-element.80) | non-fusion elementwise | flops 524288 | bytes 3145728 | tf_op jit(solution)/shard_map/convert_element_type | solution.py:22
  77.2 48.9 %all-gather.3.cloned.1.call-done = bf16[4,4096,128]{2,1,0:T(8,128)(2,1)} async-done(((bf16[1,4096,128]{2,1,0:T(8,128)(2,1)}), bf16[4,4096,128]{2,1,0:T(8,128)(2,1)}) %all-gather.3.cloned.1.call-update) | async-done | bytes 4194320 | tf_op jit(solution)/shard_map/all_gather | solution.py:22
  126.1 4.2 %fusion.72 = (bf16[1,4096,128]{2,1,0:T(8,128)(2,1)}, bf16[1,4096,128]{2,1,0:T(8,128)(2,1)}, bf16[1,4096,128]{2,1,0:T(8,128)(2,1)}, bf16[1,4096,128]{2,1,0:T(8,128)(2,1)}) fusion(bf16[4,4096,128]{2,1,0:T(8,128)(2,1)} %all-gather.3.cloned.1.call-done), kind=kLoop, calls=%fused_computation.90 | loop fusion | bytes 8388608 | tf_op jit(solution)/shard_map/slice | solution.py:26
  138.7 3.5 %fusion.45 = bf16[1,4096,128]{1,2,0:T(8,128)(2,1)} fusion(bf16[1,4096,128]{1,2,0:T(8,128)(2,1)} %copy.86, bf16[1,4096,128]{1,2,0:T(8,128)(2,1)} %copy.85, bf16[1,4096,128]{1,2,0:T(8,128)(2,1)} %copy.84, bf16[1,4096,128]{1,2,0:T(8,128)(2,1)S(1)} %copy.83), kind=kLoop, calls=%fused_computation.54 | loop fusion | flops 4194304 | bytes 5242880 | tf_op jit(solution)/shard_map/convert_element_type | solution.py:22
  144.5 48.5 %all-gather.5.cloned.1.call-done = bf16[4,4096,128]{2,1,0:T(8,128)(2,1)} async-done(((bf16[1,4096,128]{2,1,0:T(8,128)(2,1)}), bf16[4,4096,128]{2,1,0:T(8,128)(2,1)}) %all-gather.5.cloned.1.call-update) | async-done | bytes 4194320 | tf_op jit(solution)/shard_map/all_gather | solution.py:22
  193.0 4.3 %fusion.71 = (bf16[1,4096,128]{2,1,0:T(8,128)(2,1)}, bf16[1,4096,128]{2,1,0:T(8,128)(2,1)}, bf16[1,4096,128]{2,1,0:T(8,128)(2,1)}, bf16[1,4096,128]{2,1,0:T(8,128)(2,1)}) fusion(bf16[4,4096,128]{2,1,0:T(8,128)(2,1)} %all-gather.5.cloned.1.call-done), kind=kLoop, calls=%fused_computation.89 | loop fusion | bytes 8388608 | tf_op jit(solution)/shard_map/slice | solution.py:26
  206.4 6.0 %fusion.33 = f32[1,4096,128]{1,2,0:T(8,128)} fusion(bf16[1,4096,128]{1,2,0:T(8,128)(2,1)S(1)} %copy.83, bf16[1,4096,128]{1,2,0:T(8,128)(2,1)} %copy.87, bf16[1,4096,128]{1,2,0:T(8,128)(2,1)} %copy.90, bf16[1,4096,128]{1,2,0:T(8,128)(2,1)} %copy.89, bf16[1,4096,128]{1,2,0:T(8,128)(2,1)} %copy.88, bf16[1,4096,128]{1,2,0:T(8,128)(2,1)} %copy.86, ...), kind=kLoop, calls=%fused_computation.41 | loop fusion | flops 12058624 | bytes 10485768 | tf_op jit(solution)/shard_map/add | solution.py:49
  212.5 11.6 %while.25 = (s32[]{:T(128)}, f32[2,512,2,64]{1,3,2,0:T(8,128)S(1)}, f32[2,512,2,64]{1,3,2,0:T(8,128)}, f32[2,4096,2,64]{1,3,2,0:T(8,128)}, f32[4096,2,64]{0,2,1:...) while((s32[]{:T(128)}, f32[2,512,2,64]{1,3,2,0:T(8,128)S(1)}, f32[2,512,2,64]{1,3,2,0:T(8,128)}, ...), condition=%wide.region_4.5_spmd, body=%wide.region_3.4_spmd.sunk | while | flops 546439168 | bytes 49415332 | solution.py:102
  213.5 3.3 %multiply_convert_fusion.10 = bf16[512,2,64,64]{0,3,2,1:T(8,128)(2,1)S(1)} fusion(f32[512,2,64]{0,2,1:T(8,128)S(1)} %bitcast_convert_fusion.4), kind=kLoop, calls=%fused_computation.1.clone.1 | loop fusion | flops 8388608 | bytes 8650752 | tf_op jit(solution)/shard_map/while/body/eval_jaxpr/convert_element_type | solution.py:45
  219.3 3.3 %multiply_convert_fusion.10 = bf16[512,2,64,64]{0,3,2,1:T(8,128)(2,1)S(1)} fusion(f32[512,2,64]{0,2,1:T(8,128)S(1)} %bitcast_convert_fusion.4), kind=kLoop, calls=%fused_computation.1.clone.1 | loop fusion | flops 8388608 | bytes 8650752 | tf_op jit(solution)/shard_map/while/body/eval_jaxpr/convert_element_type | solution.py:45
  227.3 11.4 %all_to_all.64 = bf16[8,128,128]{1,2,0:T(8,128)(2,1)S(1)} all-to-all(bf16[8,128,128]{1,2,0:T(8,128)(2,1)S(1)} %copy.76), channel_id=1, replica_groups=mesh['aa_0'=4,'aa_1'=4,'ba'=8] {'ba'}, dimensions={0} | all-to-all | bytes 524288 | tf_op jit(solution)/shard_map/all_to_all | solution.py:108
  240.1 9.2 %fusion.46 = bf16[128,1024]{1,0:T(8,128)(2,1)} fusion(f32[128,1024]{1,0:T(8,128)S(1)} %get-tuple-element.207, bf16[4096,1024]{1,0:T(8,128)(2,1)} %param.23, bf16[1024,4096]{1,0:T(8,128)(2,1)} %param.22, f32[1024]{0:T(1024)S(1)} %copy-done.10, f32[128]{0:T(128)S(1)} %add_rsqrt_fusion.1), kind=kOutput, calls=%fused_computation.58 | convolution fusion | flops 2152857600 | bytes 17568256 | tf_op jit(solution)/shard_map/dot_general | solution.py:117
  (89 shorter events, 54.0 us)
Async XLA Ops:
  7.2 232.3 %copy-start = (bf16[1024,1024]{1,0:T(8,128)(2,1)S(1)}, bf16[1024,1024]{1,0:T(8,128)(2,1)}, u32[]{:S(2)}) copy-start(bf16[1024,1024]{1,0:T(8,128)(2,1)} %param.20) | copy-start | bytes 6291460
  7.2 10.3 %copy-start.5 = (bf16[128,1024]{1,0:T(8,128)(2,1)S(1)}, bf16[128,1024]{1,0:T(8,128)(2,1)}, u32[]{:S(2)}) copy-start(bf16[128,1024]{1,0:T(8,128)(2,1)} %param.14) | copy-start | bytes 786436
  7.2 10.3 %copy-start.8 = (f32[1024]{0:T(1024)S(1)}, f32[1024]{0:T(1024)}, u32[]{:S(2)}) copy-start(f32[1024]{0:T(1024)} %param.15) | copy-start | bytes 12292
  11.5 12.4 %all-to-all-start.2 = ((bf16[128,8,128]{0,2,1:T(8,128)(2,1)}), bf16[128,8,128]{0,2,1:T(8,128)(2,1)S(1)}, u32[]{:S(2)}, u32[]{:S(2)}) async-start(bf16[128,8,128]{0,2,1:T(8,128)(2,1)} %bitcast.11), calls=%async_computation.2 | async-start | bytes 524288 | tf_op jit(solution)/shard_map/all_to_all | solution.py:58
  23.9 10.9 %all-to-all-start = ((bf16[128,8,128]{0,2,1:T(8,128)(2,1)}), bf16[128,8,128]{0,2,1:T(8,128)(2,1)S(1)}, u32[]{:S(2)}, u32[]{:S(2)}) async-start(bf16[128,8,128]{0,2,1:T(8,128)(2,1)} %bitcast.7), calls=%async_computation | async-start | bytes 524288 | tf_op jit(solution)/shard_map/all_to_all | solution.py:60
  34.8 10.9 %all-to-all-start.1 = ((bf16[128,8,128]{0,2,1:T(8,128)(2,1)}), bf16[128,8,128]{0,2,1:T(8,128)(2,1)S(1)}, u32[]{:S(2)}, u32[]{:S(2)}) async-start(bf16[128,8,128]{0,2,1:T(8,128)(2,1)} %bitcast.9), calls=%async_computation.1 | async-start | bytes 524288 | tf_op jit(solution)/shard_map/all_to_all | solution.py:59
  39.1 87.0 %all-gather.3.cloned.1.call-start = ((), (), s32[]{:S(2)}) async-start(), calls=%async_computation.4 | async-start | bytes 5242880 | tf_op jit(solution)/shard_map/all_gather | solution.py:22
  49.2 3.3 %copy-start.1 = (f32[4096,2,64]{0,2,1:T(8,128)S(1)}, f32[4096,2,64]{0,2,1:T(8,128)}, u32[]{:S(2)}) copy-start(f32[4096,2,64]{0,2,1:T(8,128)} %get-tuple-element.298) | copy-start | bytes 6291460 | tf_op jit(solution)/shard_map/while
  55.3 1.4 copy-start.2
  62.5 3.3 %copy-start.1 = (f32[4096,2,64]{0,2,1:T(8,128)S(1)}, f32[4096,2,64]{0,2,1:T(8,128)}, u32[]{:S(2)}) copy-start(f32[4096,2,64]{0,2,1:T(8,128)} %get-tuple-element.298) | copy-start | bytes 6291460 | tf_op jit(solution)/shard_map/while
  68.6 1.4 copy-start.2
  71.8 5.2 %copy-start.6 = (f32[2,512,2,64]{1,3,2,0:T(8,128)}, f32[2,512,2,64]{1,3,2,0:T(8,128)S(1)}, u32[]{:S(2)}) copy-start(f32[2,512,2,64]{1,3,2,0:T(8,128)S(1)} %get-tuple-element.317) | copy-start | bytes 1572868
  77.0 116.0 %all-gather.5.cloned.1.call-start = ((), (), s32[]{:S(2)}) async-start(), calls=%async_computation.5 | async-start | bytes 5242880 | tf_op jit(solution)/shard_map/all_gather | solution.py:22
  213.5 3.3 %copy-start.3 = (f32[4096,2,64]{0,2,1:T(8,128)S(1)}, f32[4096,2,64]{0,2,1:T(8,128)}, u32[]{:S(2)}) copy-start(f32[4096,2,64]{0,2,1:T(8,128)} %get-tuple-element.333) | copy-start | bytes 6291460 | tf_op jit(solution)/shard_map/while
  213.5 3.3 %copy-start.4 = (f32[2,4096,2,64]{1,3,2,0:T(8,128)S(1)}, f32[2,4096,2,64]{1,3,2,0:T(8,128)}, u32[]{:S(2)}) copy-start(f32[2,4096,2,64]{1,3,2,0:T(8,128)} %get-tuple-element.332) | copy-start | bytes 12582916 | tf_op jit(solution)/shard_map/while
  213.5 3.3 %copy-start.7 = (f32[2,512,2,64]{1,3,2,0:T(8,128)S(1)}, f32[2,512,2,64]{1,3,2,0:T(8,128)}, u32[]{:S(2)}) copy-start(f32[2,512,2,64]{1,3,2,0:T(8,128)} %get-tuple-element.331) | copy-start | bytes 1572868 | tf_op jit(solution)/shard_map/while
  219.2 3.3 %copy-start.3 = (f32[4096,2,64]{0,2,1:T(8,128)S(1)}, f32[4096,2,64]{0,2,1:T(8,128)}, u32[]{:S(2)}) copy-start(f32[4096,2,64]{0,2,1:T(8,128)} %get-tuple-element.333) | copy-start | bytes 6291460 | tf_op jit(solution)/shard_map/while
  219.2 3.3 %copy-start.4 = (f32[2,4096,2,64]{1,3,2,0:T(8,128)S(1)}, f32[2,4096,2,64]{1,3,2,0:T(8,128)}, u32[]{:S(2)}) copy-start(f32[2,4096,2,64]{1,3,2,0:T(8,128)} %get-tuple-element.332) | copy-start | bytes 12582916 | tf_op jit(solution)/shard_map/while
  219.3 3.3 %copy-start.7 = (f32[2,512,2,64]{1,3,2,0:T(8,128)S(1)}, f32[2,512,2,64]{1,3,2,0:T(8,128)}, u32[]{:S(2)}) copy-start(f32[2,512,2,64]{1,3,2,0:T(8,128)} %get-tuple-element.331) | copy-start | bytes 1572868 | tf_op jit(solution)/shard_map/while
  224.1 2.9 %copy-start.9 = (f32[128]{0:T(128)S(1)}, f32[128]{0:T(128)}, u32[]{:S(2)}) copy-start(f32[128]{0:T(128)} %param.19) | copy-start | bytes 1540
  227.2 12.8 %copy-start.10 = (f32[1024]{0:T(1024)S(1)}, f32[1024]{0:T(1024)}, u32[]{:S(2)}) copy-start(f32[1024]{0:T(1024)} %param.21) | copy-start | bytes 12292
Sparse Core Ops, SparseCore 0:
  77.1 48.9 all-gather.2
  144.6 48.3 all-gather.4
where the time goes:
time: 257 us; the launch traced here: 256 us
  waiting for transfers between devices  110 us (43%)
  local copies, waits for them, and re-layouts  42 us (16%)
  other arithmetic  35.6 us (14%)
  matrix products  28 us (11%)
  starting transfers between devices  14.9 us (6%)
  between operations  14.3 us (6%)
  blocking collectives  11.4 us (4%)
    all_gather x2, waiting for transfers between devices, prefix_by_axis(): pieces = lax.all_gather(subtotal.astype(jnp.bfloat16), axis)  97.4 us
    unnamed x25, local copies, waits for them, and re-layouts  20 us
    convert_element_type x4, other arithmetic, features(): return outer_features(vectors).astype(jnp.bfloat16)  13.2 us
    all_to_all x1, blocking collectives, body(): lax.all_to_all(attended_heads, 'ba', split_axis=0, concat_axis=1, tiled=T...  11.4 us
    dot_general x1, matrix products, body(): jnp.dot(hidden, w_out, preferred_element_type=jnp.float32)  9.17 us
    slice x2, local copies, waits for them, and re-layouts, prefix_by_axis(): subtotal = combine(subtotal, pieces[k].astype(shard.dtype))  8.52 us
    convert_element_type x2, other arithmetic, prefix_by_axis(): pieces = lax.all_gather(subtotal.astype(jnp.bfloat16), axis)  6.37 us
    add x1, other arithmetic, add_states(): return earlier_state + later_state  6.04 us
  transfers between devices with their start and end apart: 5, of which 5 were waited for; matrix products, arithmetic and copies ran while one was open for 3% of the time, Pallas kernels for 0%

commit v1 on v0

--- a/solution.py
+++ b/solution.py
@@ -56,7 +56,10 @@
     values_loc = jnp.dot(normed, w_value, preferred_element_type=jnp.float32).astype(jnp.bfloat16)
     queries, keys, values = (
         lax.all_to_all(query_loc, "ba", split_axis=1, concat_axis=0, tiled=True),
-        lax.all_to_all(keys_loc, "ba", split_axis=1, concat_axis=0, tiled=True),
+        jnp.concatenate(
+            lax.all_to_all(jnp.stack(jnp.split(keys_loc, lax.axis_size("ba"), axis=1)), "ba", 0, 0),
+            axis=0,
+        ),
         lax.all_to_all(values_loc, "ba", split_axis=1, concat_axis=0, tiled=True),
     )
     head_size = D // H

time: 257 us -> 261 us (1.016)
  local copies, waits for them, and re-layouts: 42 us -> 47.7 us
    unnamed x25 -> x34, local copies, waits for them, and re-layouts: 20 us -> 25 us
  transfers between devices with their start and end apart: 5 -> 5, of which waited for: 5 -> 5; matrix products, arithmetic and copies ran while one was open for 3% -> 4% of each run, Pallas kernels for 0% -> 0%
where the time goes in v1:
time: 261 us; the launch traced here: 260 us
  waiting for transfers between devices  108 us (41%)
  local copies, waits for them, and re-layouts  47.7 us (18%)
  other arithmetic  35.6 us (14%)
  matrix products  28 us (11%)
  starting transfers between devices  14.9 us (6%)
  between operations  14.3 us (5%)
  blocking collectives  11.4 us (4%)
    all_gather x2, waiting for transfers between devices, prefix_by_axis(): pieces = lax.all_gather(subtotal.astype(jnp.bfloat16), axis)  97.4 us
    unnamed x34, local copies, waits for them, and re-layouts  25 us
    convert_element_type x4, other arithmetic, features(): return outer_features(vectors).astype(jnp.bfloat16)  13.2 us
    all_to_all x1, blocking collectives, body(): lax.all_to_all(attended_heads, 'ba', split_axis=0, concat_axis=1, tiled=T...  11.4 us
    dot_general x1, matrix products, body(): jnp.dot(hidden, w_out, preferred_element_type=jnp.float32)  9.17 us
    slice x2, local copies, waits for them, and re-layouts, prefix_by_axis(): subtotal = combine(subtotal, pieces[k].astype(shard.dtype))  8.5 us
    convert_element_type x2, other arithmetic, prefix_by_axis(): pieces = lax.all_gather(subtotal.astype(jnp.bfloat16), axis)  6.38 us
    add x1, other arithmetic, add_states(): return earlier_state + later_state  6.04 us
  transfers between devices with their start and end apart: 5, of which 5 were waited for; matrix products, arithmetic and copies ran while one was open for 4% of the time, Pallas kernels for 0%

profile of v1, /device:TPU:1, one launch (start us, length us, event | category | flops | bytes accessed | tf_op | source)
XLA Modules:
  0.0 259.9 jit_solution(15991340621586540281)
XLA Ops:
  15.7 6.0 %all-to-all-start.1 = ((bf16[8,128,128]{2,1,0:T(8,128)(2,1)}), bf16[8,128,128]{2,1,0:T(8,128)(2,1)S(1)}, u32[]{:S(2)}, u32[]{:S(2)}) async-start(bf16[8,128,128]{2,1,0:T(8,128)(2,1)} %fusion.64), calls=%async_computation.1 | async-start | bytes 524288 | tf_op jit(solution)/shard_map/all_to_all | solution.py:60
  24.6 3.5 %all-to-all-done.1 = bf16[8,128,128]{2,1,0:T(8,128)(2,1)S(1)} async-done(((bf16[8,128,128]{2,1,0:T(8,128)(2,1)}), bf16[8,128,128]{2,1,0:T(8,128)(2,1)S(1)}, u32[]{:S(2)}, u32[]{:S(2)}) %all-to-all-start.1) | async-done | bytes 262176 | tf_op jit(solution)/shard_map/all_to_all | solution.py:60
  28.1 4.4 %all-to-all-start.2 = ((bf16[128,8,128]{0,2,1:T(8,128)(2,1)}), bf16[128,8,128]{0,2,1:T(8,128)(2,1)S(1)}, u32[]{:S(2)}, u32[]{:S(2)}) async-start(bf16[128,8,128]{0,2,1:T(8,128)(2,1)} %bitcast.17), calls=%async_computation.2 | async-start | bytes 524288 | tf_op jit(solution)/shard_map/all_to_all | solution.py:58
  35.4 3.6 %all-to-all-done.2 = bf16[128,8,128]{0,2,1:T(8,128)(2,1)S(1)} async-done(((bf16[128,8,128]{0,2,1:T(8,128)(2,1)}), bf16[128,8,128]{0,2,1:T(8,128)(2,1)S(1)}, u32[]{:S(2)}, u32[]{:S(2)}) %all-to-all-start.2) | async-done | bytes 262176 | tf_op jit(solution)/shard_map/all_to_all | solution.py:58
  38.9 4.4 %all-to-all-start = ((bf16[128,8,128]{0,2,1:T(8,128)(2,1)}), bf16[128,8,128]{0,2,1:T(8,128)(2,1)S(1)}, u32[]{:S(2)}, u32[]{:S(2)}) async-start(bf16[128,8,128]{0,2,1:T(8,128)(2,1)} %bitcast.7), calls=%async_computation | async-start | bytes 524288 | tf_op jit(solution)/shard_map/all_to_all | solution.py:63
  46.6 3.2 %all-to-all-done = bf16[128,8,128]{0,2,1:T(8,128)(2,1)S(1)} async-done(((bf16[128,8,128]{0,2,1:T(8,128)(2,1)}), bf16[128,8,128]{0,2,1:T(8,128)(2,1)S(1)}, u32[]{:S(2)}, u32[]{:S(2)}) %all-to-all-start) | async-done | bytes 262176 | tf_op jit(solution)/shard_map/all_to_all | solution.py:63
  50.2 25.0 %while.26 = (s32[]{:T(128)}, f32[4096,2,64]{0,2,1:T(8,128)}, f32[2,512,2,64]{1,3,2,0:T(8,128)S(1)}, f32[2,4096,2,64]{1,3,2,0:T(8,128)}, bf16[2,512,2,64]{1,3,2,0...) while((s32[]{:T(128)}, f32[4096,2,64]{0,2,1:T(8,128)}, ...), condition=%wide.region_2.3_spmd.clone, body=%wide.region_1.2_spmd.clone.sunk | while | flops 682950656 | bytes 43911844 | solution.py:89
  52.7 3.3 %multiply_convert_fusion.11 = bf16[512,2,64,64]{0,3,2,1:T(8,128)(2,1)S(1)} fusion(f32[512,2,64]{0,2,1:T(8,128)S(1)} %bitcast_convert_fusion.5), kind=kLoop, calls=%fused_computation.10.clone.1 | loop fusion | flops 8388608 | bytes 8650752 | tf_op jit(solution)/shard_map/while/body/eval_jaxpr/convert_element_type | solution.py:45
  56.0 2.8 %fusion.108 = f32[4096,2,64]{0,2,1:T(8,128)S(1)} fusion(bf16[512,2,4096]{0,2,1:T(8,128)(2,1)S(1)} %bitcast.151, f32[4096,2,64]{0,2,1:T(8,128)S(1)} %copy-done.1, pred[]{:T(512)S(6)} %compare.3, bf16[2,512,2,64]{1,3,2,0:T(8,128)(2,1)S(1)} %get-tuple-element.317, s32[]{:T(128)} %get-tuple-element.304), kind=kOutput, calls=%fused_computation.12.clone.1 | convolution fusion | flops 537919488 | bytes 12713989 | tf_op jit(solution)/shard_map/while/body/eval_jaxpr/jhf,jhd->fhd/dot_general | solution.py:82
  61.9 3.1 %bitcast_dynamic-update-slice_fusion.2 = f32[2,4096,2,64]{1,3,2,0:T(8,128)} fusion(f32[2,4096,2,64]{1,3,2,0:T(8,128)} %get-tuple-element.307, s32[]{:T(128)} %get-tuple-element.304, f32[4096,2,64]{0,2,1:T(8,128)} %get-tuple-element.305, pred[]{:T(512)S(6)} %compare.3), kind=kLoop, calls=%fused_computation.13.clone.1 | loop fusion | flops 524288 | bytes 4194817 | tf_op jit(solution)/shard_map/while/body/jit(dynamic_update_index_in_dim)/dynamic_update_slice | solution.py:89
  66.0 3.3 %multiply_convert_fusion.11 = bf16[512,2,64,64]{0,3,2,1:T(8,128)(2,1)S(1)} fusion(f32[512,2,64]{0,2,1:T(8,128)S(1)} %bitcast_convert_fusion.5), kind=kLoop, calls=%fused_computation.10.clone.1 | loop fusion | flops 8388608 | bytes 8650752 | tf_op jit(solution)/shard_map/while/body/eval_jaxpr/convert_element_type | solution.py:45
  69.3 2.8 %fusion.108 = f32[4096,2,64]{0,2,1:T(8,128)S(1)} fusion(bf16[512,2,4096]{0,2,1:T(8,128)(2,1)S(1)} %bitcast.151, f32[4096,2,64]{0,2,1:T(8,128)S(1)} %copy-done.1, pred[]{:T(512)S(6)} %compare.3, bf16[2,512,2,64]{1,3,2,0:T(8,128)(2,1)S(1)} %get-tuple-element.317, s32[]{:T(128)} %get-tuple-element.304), kind=kOutput, calls=%fused_computation.12.clone.1 | convolution fusion | flops 537919488 | bytes 12713989 | tf_op jit(solution)/shard_map/while/body/eval_jaxpr/jhf,jhd->fhd/dot_general | solution.py:82
  75.2 2.9 %convert_element_type.145 = bf16[4096,2,64]{0,2,1:T(8,128)(2,1)} convert(f32[4096,2,64]{0,2,1:T(8,128)} %get-tuple-element.80) | non-fusion elementwise | flops 524288 | bytes 3145728 | tf_op jit(solution)/shard_map/convert_element_type | solution.py:22
  80.7 48.9 %all-gather.3.cloned.1.call-done = bf16[4,4096,128]{2,1,0:T(8,128)(2,1)} async-done(((bf16[1,4096,128]{2,1,0:T(8,128)(2,1)}), bf16[4,4096,128]{2,1,0:T(8,128)(2,1)}) %all-gather.3.cloned.1.call-update) | async-done | bytes 4194320 | tf_op jit(solution)/shard_map/all_gather | solution.py:22
  129.6 4.2 %fusion.80 = (bf16[1,4096,128]{2,1,0:T(8,128)(2,1)}, bf16[1,4096,128]{2,1,0:T(8,128)(2,1)}, bf16[1,4096,128]{2,1,0:T(8,128)(2,1)}, bf16[1,4096,128]{2,1,0:T(8,128)(2,1)}) fusion(bf16[4,4096,128]{2,1,0:T(8,128)(2,1)} %all-gather.3.cloned.1.call-done), kind=kLoop, calls=%fused_computation.106 | loop fusion | bytes 8388608 | tf_op jit(solution)/shard_map/slice | solution.py:26
  142.2 3.5 %fusion.45 = bf16[1,4096,128]{1,2,0:T(8,128)(2,1)} fusion(bf16[1,4096,128]{1,2,0:T(8,128)(2,1)} %copy.86, bf16[1,4096,128]{1,2,0:T(8,128)(2,1)} %copy.85, bf16[1,4096,128]{1,2,0:T(8,128)(2,1)} %copy.84, bf16[1,4096,128]{1,2,0:T(8,128)(2,1)S(1)} %copy.83), kind=kLoop, calls=%fused_computation.54 | loop fusion | flops 4194304 | bytes 5242880 | tf_op jit(solution)/shard_map/convert_element_type | solution.py:22
  148.1 48.5 %all-gather.5.cloned.1.call-done = bf16[4,4096,128]{2,1,0:T(8,128)(2,1)} async-done(((bf16[1,4096,128]{2,1,0:T(8,128)(2,1)}), bf16[4,4096,128]{2,1,0:T(8,128)(2,1)}) %all-gather.5.cloned.1.call-update) | async-done | bytes 4194320 | tf_op jit(solution)/shard_map/all_gather | solution.py:22
  196.5 4.3 %fusion.79 = (bf16[1,4096,128]{2,1,0:T(8,128)(2,1)}, bf16[1,4096,128]{2,1,0:T(8,128)(2,1)}, bf16[1,4096,128]{2,1,0:T(8,128)(2,1)}, bf16[1,4096,128]{2,1,0:T(8,128)(2,1)}) fusion(bf16[4,4096,128]{2,1,0:T(8,128)(2,1)} %all-gather.5.cloned.1.call-done), kind=kLoop, calls=%fused_computation.105 | loop fusion | bytes 8388608 | tf_op jit(solution)/shard_map/slice | solution.py:26
  210.2 6.0 %fusion.33 = f32[1,4096,128]{1,2,0:T(8,128)} fusion(bf16[1,4096,128]{1,2,0:T(8,128)(2,1)S(1)} %copy.83, bf16[1,4096,128]{1,2,0:T(8,128)(2,1)} %copy.87, bf16[1,4096,128]{1,2,0:T(8,128)(2,1)} %copy.90, bf16[1,4096,128]{1,2,0:T(8,128)(2,1)} %copy.89, bf16[1,4096,128]{1,2,0:T(8,128)(2,1)} %copy.88, bf16[1,4096,128]{1,2,0:T(8,128)(2,1)} %copy.86, ...), kind=kLoop, calls=%fused_computation.41 | loop fusion | flops 12058624 | bytes 10485768 | tf_op jit(solution)/shard_map/add | solution.py:49
  216.3 11.6 %while.25 = (s32[]{:T(128)}, f32[2,512,2,64]{1,3,2,0:T(8,128)S(1)}, f32[2,512,2,64]{1,3,2,0:T(8,128)}, f32[2,4096,2,64]{1,3,2,0:T(8,128)}, f32[4096,2,64]{0,2,1:...) while((s32[]{:T(128)}, f32[2,512,2,64]{1,3,2,0:T(8,128)S(1)}, f32[2,512,2,64]{1,3,2,0:T(8,128)}, ...), condition=%wide.region_4.5_spmd, body=%wide.region_3.4_spmd.sunk | while | flops 546439168 | bytes 49415332 | solution.py:105
  217.3 3.3 %multiply_convert_fusion.10 = bf16[512,2,64,64]{0,3,2,1:T(8,128)(2,1)S(1)} fusion(f32[512,2,64]{0,2,1:T(8,128)S(1)} %bitcast_convert_fusion.4), kind=kLoop, calls=%fused_computation.1.clone.1 | loop fusion | flops 8388608 | bytes 8650752 | tf_op jit(solution)/shard_map/while/body/eval_jaxpr/convert_element_type | solution.py:45
  223.1 3.3 %multiply_convert_fusion.10 = bf16[512,2,64,64]{0,3,2,1:T(8,128)(2,1)S(1)} fusion(f32[512,2,64]{0,2,1:T(8,128)S(1)} %bitcast_convert_fusion.4), kind=kLoop, calls=%fused_computation.1.clone.1 | loop fusion | flops 8388608 | bytes 8650752 | tf_op jit(solution)/shard_map/while/body/eval_jaxpr/convert_element_type | solution.py:45
  231.0 11.4 %all_to_all.53 = bf16[8,128,128]{1,2,0:T(8,128)(2,1)S(1)} all-to-all(bf16[8,128,128]{1,2,0:T(8,128)(2,1)S(1)} %copy.75), channel_id=1, replica_groups=mesh['aa_0'=4,'aa_1'=4,'ba'=8] {'ba'}, dimensions={0} | all-to-all | bytes 524288 | tf_op jit(solution)/shard_map/all_to_all | solution.py:111
  243.9 9.2 %fusion.46 = bf16[128,1024]{1,0:T(8,128)(2,1)} fusion(f32[128,1024]{1,0:T(8,128)S(1)} %get-tuple-element.214, bf16[4096,1024]{1,0:T(8,128)(2,1)} %param.23, bf16[1024,4096]{1,0:T(8,128)(2,1)} %param.22, f32[1024]{0:T(1024)S(1)} %copy-done.11, f32[128]{0:T(128)S(1)} %add_rsqrt_fusion.1), kind=kOutput, calls=%fused_computation.58 | convolution fusion | flops 2152857600 | bytes 17568256 | tf_op jit(solution)/shard_map/dot_general | solution.py:120
  (97 shorter events, 59.7 us)
Async XLA Ops:
  7.2 236.1 %copy-start = (bf16[1024,1024]{1,0:T(8,128)(2,1)S(1)}, bf16[1024,1024]{1,0:T(8,128)(2,1)}, u32[]{:S(2)}) copy-start(bf16[1024,1024]{1,0:T(8,128)(2,1)} %param.20) | copy-start | bytes 6291460
  7.2 14.4 %copy-start.5 = (bf16[128,1024]{1,0:T(8,128)(2,1)S(1)}, bf16[128,1024]{1,0:T(8,128)(2,1)}, u32[]{:S(2)}) copy-start(bf16[128,1024]{1,0:T(8,128)(2,1)} %param.14) | copy-start | bytes 786436
  7.2 14.4 %copy-start.9 = (f32[1024]{0:T(1024)S(1)}, f32[1024]{0:T(1024)}, u32[]{:S(2)}) copy-start(f32[1024]{0:T(1024)} %param.15) | copy-start | bytes 12292
  15.7 12.4 %all-to-all-start.1 = ((bf16[8,128,128]{2,1,0:T(8,128)(2,1)}), bf16[8,128,128]{2,1,0:T(8,128)(2,1)S(1)}, u32[]{:S(2)}, u32[]{:S(2)}) async-start(bf16[8,128,128]{2,1,0:T(8,128)(2,1)} %fusion.64), calls=%async_computation.1 | async-start | bytes 524288 | tf_op jit(solution)/shard_map/all_to_all | solution.py:60
  28.1 10.9 %all-to-all-start.2 = ((bf16[128,8,128]{0,2,1:T(8,128)(2,1)}), bf16[128,8,128]{0,2,1:T(8,128)(2,1)S(1)}, u32[]{:S(2)}, u32[]{:S(2)}) async-start(bf16[128,8,128]{0,2,1:T(8,128)(2,1)} %bitcast.17), calls=%async_computation.2 | async-start | bytes 524288 | tf_op jit(solution)/shard_map/all_to_all | solution.py:58
  38.9 4.4 %copy-start.8 = (bf16[128,8,128]{0,2,1:T(8,128)(2,1)}, bf16[128,8,128]{0,2,1:T(8,128)(2,1)S(1)}, u32[]{:S(2)}) copy-start(bf16[128,8,128]{0,2,1:T(8,128)(2,1)S(1)} %all-to-all-done.2) | copy-start | bytes 786436
  38.9 10.9 %all-to-all-start = ((bf16[128,8,128]{0,2,1:T(8,128)(2,1)}), bf16[128,8,128]{0,2,1:T(8,128)(2,1)S(1)}, u32[]{:S(2)}, u32[]{:S(2)}) async-start(bf16[128,8,128]{0,2,1:T(8,128)(2,1)} %bitcast.7), calls=%async_computation | async-start | bytes 524288 | tf_op jit(solution)/shard_map/all_to_all | solution.py:63
  43.3 86.3 %all-gather.3.cloned.1.call-start = ((), (), s32[]{:S(2)}) async-start(), calls=%async_computation.4 | async-start | bytes 5242880 | tf_op jit(solution)/shard_map/all_gather | solution.py:22
  52.7 3.3 %copy-start.1 = (f32[4096,2,64]{0,2,1:T(8,128)S(1)}, f32[4096,2,64]{0,2,1:T(8,128)}, u32[]{:S(2)}) copy-start(f32[4096,2,64]{0,2,1:T(8,128)} %get-tuple-element.305) | copy-start | bytes 6291460 | tf_op jit(solution)/shard_map/while
  58.7 1.4 copy-start.2
  66.0 3.3 %copy-start.1 = (f32[4096,2,64]{0,2,1:T(8,128)S(1)}, f32[4096,2,64]{0,2,1:T(8,128)}, u32[]{:S(2)}) copy-start(f32[4096,2,64]{0,2,1:T(8,128)} %get-tuple-element.305) | copy-start | bytes 6291460 | tf_op jit(solution)/shard_map/while
  72.0 1.4 copy-start.2
  75.2 5.2 %copy-start.6 = (f32[2,512,2,64]{1,3,2,0:T(8,128)}, f32[2,512,2,64]{1,3,2,0:T(8,128)S(1)}, u32[]{:S(2)}) copy-start(f32[2,512,2,64]{1,3,2,0:T(8,128)S(1)} %get-tuple-element.324) | copy-start | bytes 1572868
  80.5 116.1 %all-gather.5.cloned.1.call-start = ((), (), s32[]{:S(2)}) async-start(), calls=%async_computation.5 | async-start | bytes 5242880 | tf_op jit(solution)/shard_map/all_gather | solution.py:22
  217.2 3.3 %copy-start.3 = (f32[4096,2,64]{0,2,1:T(8,128)S(1)}, f32[4096,2,64]{0,2,1:T(8,128)}, u32[]{:S(2)}) copy-start(f32[4096,2,64]{0,2,1:T(8,128)} %get-tuple-element.340) | copy-start | bytes 6291460 | tf_op jit(solution)/shard_map/while
  217.3 3.3 %copy-start.4 = (f32[2,4096,2,64]{1,3,2,0:T(8,128)S(1)}, f32[2,4096,2,64]{1,3,2,0:T(8,128)}, u32[]{:S(2)}) copy-start(f32[2,4096,2,64]{1,3,2,0:T(8,128)} %get-tuple-element.339) | copy-start | bytes 12582916 | tf_op jit(solution)/shard_map/while
  217.3 3.3 %copy-start.7 = (f32[2,512,2,64]{1,3,2,0:T(8,128)S(1)}, f32[2,512,2,64]{1,3,2,0:T(8,128)}, u32[]{:S(2)}) copy-start(f32[2,512,2,64]{1,3,2,0:T(8,128)} %get-tuple-element.338) | copy-start | bytes 1572868 | tf_op jit(solution)/shard_map/while
  223.0 3.3 %copy-start.3 = (f32[4096,2,64]{0,2,1:T(8,128)S(1)}, f32[4096,2,64]{0,2,1:T(8,128)}, u32[]{:S(2)}) copy-start(f32[4096,2,64]{0,2,1:T(8,128)} %get-tuple-element.340) | copy-start | bytes 6291460 | tf_op jit(solution)/shard_map/while
  223.0 3.3 %copy-start.4 = (f32[2,4096,2,64]{1,3,2,0:T(8,128)S(1)}, f32[2,4096,2,64]{1,3,2,0:T(8,128)}, u32[]{:S(2)}) copy-start(f32[2,4096,2,64]{1,3,2,0:T(8,128)} %get-tuple-element.339) | copy-start | bytes 12582916 | tf_op jit(solution)/shard_map/while
  223.0 3.3 %copy-start.7 = (f32[2,512,2,64]{1,3,2,0:T(8,128)S(1)}, f32[2,512,2,64]{1,3,2,0:T(8,128)}, u32[]{:S(2)}) copy-start(f32[2,512,2,64]{1,3,2,0:T(8,128)} %get-tuple-element.338) | copy-start | bytes 1572868 | tf_op jit(solution)/shard_map/while
  227.9 2.9 %copy-start.10 = (f32[128]{0:T(128)S(1)}, f32[128]{0:T(128)}, u32[]{:S(2)}) copy-start(f32[128]{0:T(128)} %param.19) | copy-start | bytes 1540
  231.0 12.8 %copy-start.11 = (f32[1024]{0:T(1024)S(1)}, f32[1024]{0:T(1024)}, u32[]{:S(2)}) copy-start(f32[1024]{0:T(1024)} %param.21) | copy-start | bytes 12292
Sparse Core Ops, SparseCore 0:
  80.6 48.9 all-gather.2
  148.2 48.3 all-gather.4
